TPU v7x, 256 devices: a whole 4x4x8 slice. The times are simulated.
256 devices in a mesh: tm: 64 (over y, z, core), region: 4 (over x).
Axes of the slice: x: 4, y: 4, z: 8, core: 2. Of those that a mesh axis runs over, the one named last changes fastest.
Arguments:
- covariates: bfloat16 [8, 8192, 256], P('region', 'tm'), may hold values from -4 to 4
- observed: float32 [8, 8192, 256], P('region', 'tm'), may hold values from -40 to 40
- input_weight: bfloat16 [256, 256], replicated, may hold values from -0.375 to 0.375
- filter_weight: bfloat16 [3, 512, 512], replicated, may hold values from -0.25 to 0.25
- mixing_weight: bfloat16 [3, 256, 256], replicated, may hold values from -0.375 to 0.375
- output_weight: bfloat16 [256, 4096], replicated, may hold values from -0.375 to 0.375
Outputs:
- covariate_grad: bfloat16 [8, 8192, 256], P('region', 'tm')
- input_grad: bfloat16 [256, 256], P('tm')
- filter_grad: bfloat16 [3, 512, 512], P(None, 'tm')
- mixing_grad: bfloat16 [3, 256, 256], P(None, 'tm')
- output_grad: bfloat16 [256, 4096], P('tm')
All inputs are finite; a program needn't handle non-finite values.
Results may differ from a plain program's by a relative error of at most 0.022.
Values may be sent and summed in bfloat16 or wider, within the bound.
No kernel may reach another device: no remote copies, remote signals or barrier semaphores. Data moves between devices by JAX's collectives and lax.ppermute only.
A program may use at most 64 MiB of HBM per device.

v0:
```python
import jax
import jax.numpy as jnp
from jax import lax
from jax.sharding import PartitionSpec as P

epsilon = 1e-05


def passed_along(block, axis, distance):
    devices = range(lax.axis_size(axis))
    route = [(i - distance, i) for i in devices if i - distance in devices]
    return lax.ppermute(block, axis, route)


def energy(predicted, observed, scenarios):
    node_count = observed.shape[-1]
    scenario_vals = predicted.reshape(predicted.shape[:-1] + (scenarios, node_count))
    gram_matrix = jnp.einsum(
        "...sn,...rn->...sr", scenario_vals, scenario_vals, precision=lax.Precision.HIGHEST
    )
    against = jnp.einsum(
        "...sn,...n->...s", scenario_vals, observed, precision=lax.Precision.HIGHEST
    )
    own_sq = jnp.diagonal(gram_matrix, axis1=-2, axis2=-1)
    target = jnp.sum(observed * observed, axis=-1)
    to_target = jnp.sqrt((own_sq - 2.0 * against + target[..., None]) / node_count + epsilon)
    off_diag = 1.0 - jnp.eye(scenarios, dtype=jnp.float32)
    pair_sq = (own_sq[..., :, None] + own_sq[..., None, :] - 2.0 * gram_matrix) / node_count
    between = jnp.sqrt(pair_sq * off_diag + epsilon) * off_diag
    return jnp.mean(to_target, axis=-1) - jnp.sum(between, axis=(-2, -1)) / (
        2.0 * scenarios * (scenarios - 1)
    )


def layer_forward(hidden, delayed, w_filter, w_mixing):
    channels = hidden.shape[-1]
    joined = jnp.concatenate([delayed, hidden], axis=-1)
    preact = jnp.dot(joined, w_filter, preferred_element_type=jnp.float32)
    gated = (jnp.tanh(preact[..., :channels]) * jax.nn.sigmoid(preact[..., channels:])).astype(
        jnp.bfloat16
    )
    result = (
        hidden.astype(jnp.float32) + jnp.dot(gated, w_mixing, preferred_element_type=jnp.float32)
    ).astype(jnp.bfloat16)
    return (result, (joined, preact, gated))


def layer_backward(grad_out, stored_layer, w_filter, w_mixing):
    joined, preact, gated = stored_layer
    channels = gated.shape[-1]
    upstream = grad_out.astype(jnp.float32)
    grad_mixing = jnp.einsum("btc,btd->cd", gated, upstream, preferred_element_type=jnp.float32)
    gated_cot = jnp.dot(upstream, w_mixing.T, preferred_element_type=jnp.float32).astype(
        jnp.bfloat16
    )
    grad_gated = lax.optimization_barrier(gated_cot).astype(jnp.float32)
    filter_act = jnp.tanh(preact[..., :channels])
    gate_act = jax.nn.sigmoid(preact[..., channels:])
    grad_preact = jnp.concatenate(
        [
            grad_gated * gate_act * (1.0 - filter_act * filter_act),
            grad_gated * filter_act * gate_act * (1.0 - gate_act),
        ],
        axis=-1,
    )
    grad_filter = jnp.einsum("btk,btj->kj", joined, grad_preact, preferred_element_type=jnp.float32)
    grad_joined = jnp.dot(grad_preact, w_filter.T, preferred_element_type=jnp.float32).astype(
        jnp.bfloat16
    )
    return (
        grad_joined[..., :channels],
        grad_joined[..., channels:],
        grad_out,
        grad_filter,
        grad_mixing,
    )


def per_device(covariates, observed, input_weight, filter_weight, mixing_weight, output_weight):
    batch_seqs, row_count, node_count = covariates.shape
    layer_total = filter_weight.shape[0]
    channels = mixing_weight.shape[1]
    scenarios = output_weight.shape[1] // node_count
    length = row_count * lax.axis_size("tm")
    local_sq = jnp.sum(observed * observed, axis=(1, 2))
    total_sq = lax.psum(local_sq, "tm")
    inv_scale = 1.0 / jnp.sqrt(total_sq / (length * node_count) + epsilon)
    hidden = jnp.dot(covariates, input_weight, preferred_element_type=jnp.float32).astype(
        jnp.bfloat16
    )
    stored = []
    for layer_no in range(layer_total):
        dilation = 2**layer_no
        incoming = passed_along(hidden[:, row_count - dilation :, :], "tm", 1)
        delayed = jnp.concatenate([incoming, hidden[:, : row_count - dilation, :]], axis=1)
        hidden, stored_layer = layer_forward(
            hidden, delayed, filter_weight[layer_no], mixing_weight[layer_no]
        )
        stored.append(stored_layer)
    predicted = jnp.dot(hidden, output_weight, preferred_element_type=jnp.float32)

    def scoring(values):
        return jnp.sum(energy(values, observed, scenarios) * inv_scale[:, None])

    _, pull_back = jax.vjp(scoring, predicted)
    (grad_pred,) = pull_back(jnp.ones((), jnp.float32))
    grad_output = jnp.einsum("btc,btj->cj", hidden, grad_pred, preferred_element_type=jnp.float32)
    grad_last = jnp.dot(grad_pred, output_weight.T, preferred_element_type=jnp.float32).astype(
        jnp.bfloat16
    )
    grad_hidden = grad_last
    filter_parts = [None] * layer_total
    mixing_parts = [None] * layer_total
    for layer_no in reversed(range(layer_total)):
        dilation = 2**layer_no
        grad_past, grad_now, grad_resid, grad_filter, grad_mixing = layer_backward(
            grad_hidden, stored[layer_no], filter_weight[layer_no], mixing_weight[layer_no]
        )
        extent = grad_past.shape[1]
        inside = jnp.concatenate(
            [grad_past[:, dilation:, :], jnp.zeros((batch_seqs, dilation, channels), jnp.bfloat16)],
            axis=1,
        )
        grad_hidden = grad_resid + grad_now + inside
        returned = passed_along(grad_past[:, :dilation, :], "tm", -1)
        grad_hidden = grad_hidden + jnp.concatenate(
            [jnp.zeros((batch_seqs, extent - dilation, channels), jnp.bfloat16), returned], axis=1
        )
        filter_parts[layer_no] = grad_filter
        mixing_parts[layer_no] = grad_mixing
    grad_input = jnp.einsum(
        "btn,btc->nc", covariates, grad_hidden, preferred_element_type=jnp.float32
    )
    covariate_grad = jnp.dot(
        grad_hidden, input_weight.T, preferred_element_type=jnp.float32
    ).astype(jnp.bfloat16)
    grad_filters = jnp.stack(filter_parts)
    grad_mixings = jnp.stack(mixing_parts)
    shares = (
        lax.psum_scatter(grad_input, "tm", scatter_dimension=0, tiled=True),
        lax.psum_scatter(grad_filters, "tm", scatter_dimension=1, tiled=True),
        lax.psum_scatter(grad_mixings, "tm", scatter_dimension=1, tiled=True),
        lax.psum_scatter(grad_output, "tm", scatter_dimension=0, tiled=True),
    )
    shares = (
        lax.psum(shares[0].astype(jnp.bfloat16), "region").astype(jnp.float32),
        lax.psum(shares[1].astype(jnp.bfloat16), "region").astype(jnp.float32),
        lax.psum(shares[2].astype(jnp.bfloat16), "region").astype(jnp.float32),
        lax.psum(shares[3].astype(jnp.bfloat16), "region").astype(jnp.float32),
    )
    shares = tuple((piece.astype(jnp.bfloat16) for piece in shares))
    return (covariate_grad, shares[0], shares[1], shares[2], shares[3])


def solution(mesh):
    placed = (P("region", "tm", None), P("region", "tm", None), P(), P(), P(), P())
    return jax.shard_map(
        per_device,
        mesh=mesh,
        in_specs=placed,
        out_specs=(
            P("region", "tm", None),
            P("tm", None),
            P(None, "tm", None),
            P(None, "tm", None),
            P("tm", None),
        ),
        check_vma=False,
    )
```

profile of v0, /device:TPU:8, one launch (start us, length us, event | category | flops | bytes accessed | tf_op | source)
XLA Modules:
  0.0 587.4 jit_solution(2315299154174542685)
XLA Ops:
  8.5 1.9 collective-permute-start
  12.2 109.8 %psum.35 = f32[2]{0:T(128)S(1)} all-reduce(f32[2]{0:T(128)S(1)} %get-tuple-element.28), channel_id=1, replica_groups=mesh['tm'=64,'region'=4] {'tm'}, use_global_device_ids=true, to_apply=%region_2.3 | all-reduce | flops 2 | bytes 16 | tf_op jit(solution)/shard_map/psum | solution.py:86
  125.9 1.9 collective-permute-start.1
  128.4 4.6 collective-permute-done.1
  134.2 1.9 collective-permute-start.2
  136.6 4.6 collective-permute-done.2
  143.9 1.7 copy.97
  145.7 1.9 copy-done.1
  147.6 6.3 %fusion.6 = f32[2,128,16,16]{3,2,1,0:T(8,128)} fusion(f32[2,128,16,256]{3,2,1,0:T(8,128)S(1)} %bitcast.162), kind=kOutput, calls=%fused_computation.9 | convolution fusion | flops 201326592 | bytes 4456448 | tf_op jit(solution)/shard_map/jvp(...sn,...rn->...sr)/dot_general | solution.py:18
  153.9 3.2 copy.60
  157.2 2.3 copy.63
  161.8 6.5 %fusion.4 = f32[2,128,1,16]{3,2,1,0:T(1,128)} fusion(f32[2,128,256,1]{2,1,0,3:T(8,128)S(1)} %bitcast.167, f32[2,128,16,256]{3,2,1,0:T(8,128)} %bitcast.163), kind=kOutput, calls=%fused_computation.7 | convolution fusion | flops 12582912 | bytes 4472832 | tf_op jit(solution)/shard_map/jvp(...sn,...n->...s)/dot_general | solution.py:21
  174.1 2.1 copy.71
  176.3 6.9 %fusion = f32[2,128,16,256]{3,2,1,0:T(8,128)S(1)} fusion(f32[2,128,16,16]{3,2,1,0:T(8,128)} %copy.71, f32[2,128,16,256]{3,2,1,0:T(8,128)} %bitcast.164), kind=kOutput, calls=%fused_computation.3 | convolution fusion | flops 201326592 | bytes 8650752 | tf_op jit(solution)/shard_map/transpose(jvp(...sn,...rn->...sr))/dot_general | solution.py:18
  183.2 5.7 add_add_fusion
  188.9 4.2 reshape.36
  193.1 2.5 fusion.17
  196.4 1.9 collective-permute-start.3
  200.5 5.7 collective-permute-start.4
  208.6 2.0 pad_maximum_fusion
  212.5 4.3 convolution_bitcast_fusion
  218.8 5.7 collective-permute-start.5
  226.1 264.1 %all-reduce.15 = (bf16[256,256]{0,1:T(8,128)(2,1)S(1)}, bf16[3,256,256]{2,1,0:T(8,128)(2,1)}, bf16[256,4096]{1,0:T(8,128)(2,1)}) all-reduce(f32[256,256]{0,1:T(8,128)S(1)} %convolution_bitcast_fusion.7, f32[3,256,256]{2,1,0:T(8,128)S(1)} %pad_maximum_fusion.1, ...), channel_id=2, replica_groups=mesh['tm'=64,'region'=4] {'tm'}, use_global_device_ids=true, to_apply=%region_6.7.clone | all-reduce | flops 1310720 | bytes 7864320
  496.1 79.0 %all-reduce.14.cloned.1.call-done = (bf16[4,256]{0,1:T(8,128)(2,1)}, bf16[3,8,512]{2,1,0:T(8,128)(2,1)}, bf16[3,4,256]{2,1,0:T(4,128)(2,1)}, bf16[4,4096]{1,0:T(4,128)(2,1)}) async-done(((bf16[4,256]{0,1:T(8,128)(2,1)}, bf16[3,8,512]{2,1,0:T(8,128)(2,1)}, bf16[3,4,256]{2,1,0:T(4,128)(2,1)}, bf16[4,4096]{1,0:T(4,128)(2,1)}), (bf16[4,256]{0,1:T(8,128)(2,1)}, bf16[3,8,512]{2,1,0:T(8,128)(2,1)}, ...) | async-done | bytes 65552 | tf_op jit(solution)/shard_map/psum | solution.py:146
  (138 shorter events, 41.1 us)
Async XLA Ops:
  7.2 136.0 %copy-start = (bf16[256,4096]{1,0:T(8,128)(2,1)S(1)}, bf16[256,4096]{1,0:T(8,128)(2,1)}, u32[]{:S(2)}) copy-start(bf16[256,4096]{1,0:T(8,128)(2,1)} %param.11) | copy-start | bytes 6291460
  7.2 486.6 %reduce-scatter.4.cloned.1.call-start = ((), (), s32[]{:S(2)}) async-start(), calls=%async_computation.1 | async-start | bytes 3194880 | tf_op jit(solution)/shard_map/reduce_scatter | solution.py:141
  8.5 114.7 %collective-permute-start = (bf16[2,1,256]{2,1,0:T(2,128)(2,1)S(1)}, bf16[2,1,256]{2,1,0:T(2,128)(2,1)S(1)}, u32[]{:S(2)}, u32[]{:S(2)}) collective-permute-start(bf16[2,1,256]{2,1,0:T(2,128)(2,1)S(1)} %slice.133), channel_id=1, source_target_pairs={{0,4},{4,8},{8,12},{12,16},{16,20},{20,24},{24,28},{28,32},{32,36}... | collective-permute-start | bytes 3080 | tf_op jit(solution)/shard_map/ppermute | solution.py:12
  122.0 11.5 %copy-start.30 = (bf16[3,512,512]{2,1,0:T(8,128)(2,1)S(1)}, bf16[3,512,512]{2,1,0:T(8,128)(2,1)}, u32[]{:S(2)}) copy-start(bf16[3,512,512]{2,1,0:T(8,128)(2,1)} %param.9) | copy-start | bytes 4718596
  123.2 10.7 %copy-start.9 = (bf16[3,256,256]{2,1,0:T(8,128)(2,1)S(1)}, bf16[3,256,256]{2,1,0:T(8,128)(2,1)}, u32[]{:S(2)}) copy-start(bf16[3,256,256]{2,1,0:T(8,128)(2,1)} %param.10) | copy-start | bytes 1179652
  124.7 8.2 %copy-start.13 = (bf16[2,128,256]{2,1,0:T(8,128)(2,1)}, bf16[2,128,256]{2,1,0:T(8,128)(2,1)S(1)}, u32[]{:S(2)}) copy-start(bf16[2,128,256]{2,1,0:T(8,128)(2,1)S(1)} %multiply_convert_fusion.2) | copy-start | bytes 393220
  125.9 7.0 %collective-permute-start.1 = (bf16[2,2,256]{2,1,0:T(2,128)(2,1)S(1)}, bf16[2,2,256]{2,1,0:T(2,128)(2,1)S(1)}, u32[]{:S(2)}, u32[]{:S(2)}) collective-permute-start(bf16[2,2,256]{2,1,0:T(2,128)(2,1)S(1)} %slice.137), channel_id=1, source_target_pairs={{0,4},{4,8},{8,12},{12,16},{16,20},{20,24},{24,28},{28,32},{32,36}... | collective-permute-start | bytes 6152 | tf_op jit(solution)/shard_map/ppermute | solution.py:12
  133.8 7.8 %copy-start.5 = (f32[2,128,512]{2,1,0:T(8,128)}, f32[2,128,512]{2,1,0:T(8,128)S(1)}, u32[]{:S(2)}) copy-start(f32[2,128,512]{2,1,0:T(8,128)S(1)} %fusion.24) | copy-start | bytes 1572868
  134.0 7.3 %copy-start.15 = (bf16[2,128,256]{2,1,0:T(8,128)(2,1)}, bf16[2,128,256]{2,1,0:T(8,128)(2,1)S(1)}, u32[]{:S(2)}) copy-start(bf16[2,128,256]{2,1,0:T(8,128)(2,1)S(1)} %multiply_convert_fusion.1) | copy-start | bytes 393220
  134.2 7.0 %collective-permute-start.2 = (bf16[2,4,256]{2,1,0:T(4,128)(2,1)S(1)}, bf16[2,4,256]{2,1,0:T(4,128)(2,1)S(1)}, u32[]{:S(2)}, u32[]{:S(2)}) collective-permute-start(bf16[2,4,256]{2,1,0:T(4,128)(2,1)S(1)} %slice.141), channel_id=1, source_target_pairs={{0,4},{4,8},{8,12},{12,16},{16,20},{20,24},{24,28},{28,32},{32,36}... | collective-permute-start | bytes 12296 | tf_op jit(solution)/shard_map/ppermute | solution.py:12
  153.9 7.8 %copy-start.4 = (f32[2,128,256]{2,1,0:T(8,128)S(1)}, f32[2,128,256]{2,1,0:T(8,128)}, u32[]{:S(2)}) copy-start(f32[2,128,256]{2,1,0:T(8,128)} %param.7) | copy-start | bytes 786436
  176.3 6.9 %copy-start.2 = (f32[32,8,16,256]{3,2,1,0:T(8,128)S(1)}, f32[32,8,16,256]{3,2,1,0:T(8,128)}, u32[]{:S(2)}) copy-start(f32[32,8,16,256]{3,2,1,0:T(8,128)} %copy-done.1) | copy-start | bytes 12582916
  176.3 6.9 %copy-start.3 = (f32[2,128,16,16]{3,2,1,0:T(8,128)S(1)}, f32[2,128,16,16]{3,2,1,0:T(8,128)}, u32[]{:S(2)}) copy-start(f32[2,128,16,16]{3,2,1,0:T(8,128)} %copy.71) | copy-start | bytes 786436
  196.4 3.2 collective-permute-start.3
  198.7 7.5 %copy-start.29 = (bf16[2,2,256]{2,1,0:T(2,128)(2,1)S(1)}, bf16[2,2,256]{2,1,0:T(2,128)(2,1)}, u32[]{:S(2)}) copy-start(bf16[2,2,256]{2,1,0:T(2,128)(2,1)} %copy-done.28) | copy-start | bytes 6148
  200.4 7.5 %copy-start.27 = (bf16[2,1,256]{2,1,0:T(2,128)(2,1)S(1)}, bf16[2,1,256]{2,1,0:T(2,128)(2,1)}, u32[]{:S(2)}) copy-start(bf16[2,1,256]{2,1,0:T(2,128)(2,1)} %copy-done.26) | copy-start | bytes 3076
  200.5 7.0 %collective-permute-start.4 = (bf16[2,2,256]{2,1,0:T(2,128)(2,1)S(1)}, bf16[2,2,256]{2,1,0:T(2,128)(2,1)S(1)}, u32[]{:S(2)}, u32[]{:S(2)}) collective-permute-start(bf16[2,2,256]{2,1,0:T(2,128)(2,1)S(1)} %slice.150), channel_id=1, source_target_pairs={{4,0},{8,4},{12,8},{16,12},{20,16},{24,20},{28,24},{32,28},{36,32}... | collective-permute-start | bytes 6152 | tf_op jit(solution)/shard_map/ppermute | solution.py:12
  210.6 364.5 %all-reduce.14.cloned.1.call-start = ((), (), s32[]{:S(2)}) async-start(), calls=%async_computation.2 | async-start | bytes 258048 | tf_op jit(solution)/shard_map/psum | solution.py:146
  212.5 4.6 copy-start.16
  212.5 4.8 copy-start.21
  216.9 7.6 %copy-start.14 = (bf16[2,128,256]{2,1,0:T(8,128)(2,1)S(1)}, bf16[2,128,256]{2,1,0:T(8,128)(2,1)}, u32[]{:S(2)}) copy-start(bf16[2,128,256]{2,1,0:T(8,128)(2,1)} %copy-done.13) | copy-start | bytes 393220
  217.3 8.5 %copy-start.22 = (bf16[2,128,256]{2,1,0:T(8,128)(2,1)S(1)}, bf16[2,128,256]{2,1,0:T(8,128)(2,1)}, u32[]{:S(2)}) copy-start(bf16[2,128,256]{2,1,0:T(8,128)(2,1)} %param.6) | copy-start | bytes 393220
  218.8 7.0 %collective-permute-start.5 = (bf16[2,1,256]{2,1,0:T(2,128)(2,1)S(1)}, bf16[2,1,256]{2,1,0:T(2,128)(2,1)S(1)}, u32[]{:S(2)}, u32[]{:S(2)}) collective-permute-start(bf16[2,1,256]{2,1,0:T(2,128)(2,1)S(1)} %slice.153), channel_id=1, source_target_pairs={{4,0},{8,4},{12,8},{16,12},{20,16},{24,20},{28,24},{32,28},{36,32}... | collective-permute-start | bytes 3080 | tf_op jit(solution)/shard_map/ppermute | solution.py:12
  226.1 269.1 %copy-start.19 = (bf16[256,256]{1,0:T(8,128)(2,1)S(1)}, bf16[256,256]{1,0:T(8,128)(2,1)}, u32[]{:S(2)}) copy-start(bf16[256,256]{1,0:T(8,128)(2,1)} %param.8) | copy-start | bytes 393220
  (17 other events, 31.2 us)
Sparse Core Ops, SparseCore 0:
  210.7 148.8 reduce-scatter.3
  495.3 79.7 all-reduce.13
where the time goes:
time: 589 us; the launch traced here: 587 us
  blocking collectives  374 us (63%)
  waiting for transfers between devices  91 us (15%)
  matrix products  43.1 us (7%)
  local copies, waits for them, and re-layouts  32.3 us (5%)
  starting transfers between devices  19.2 us (3%)
  between operations  15.4 us (3%)
  other arithmetic  12.4 us (2%)
    unnamed x1, blocking collectives  264 us
    psum x1, blocking collectives, per_device(): total_sq = lax.psum(local_sq, 'tm')  110 us
    psum x1, waiting for transfers between devices, per_device(): lax.psum(shares[0].astype(jnp.bfloat16), 'region').astype(jnp.float32)  79 us
    ppermute x6, starting transfers between devices, passed_along(): return lax.ppermute(block, axis, route)  19.1 us
    dot_general x3, matrix products, energy(): jnp.einsum('...sn,...rn->...sr', scenario_vals, scenario_vals, precision=...  18.9 us
    unnamed x72, local copies, waits for them, and re-layouts  12.7 us
    ppermute x6, waiting for transfers between devices, passed_along(): return lax.ppermute(block, axis, route)  11.9 us
  transfers between devices with their start and end apart: 8, of which 6 were waited for; matrix products, arithmetic and copies ran while one was open for 3% of the time, Pallas kernels for 0%

commit v1 on v0

--- a/solution.py
+++ b/solution.py
@@ -143,7 +143,9 @@
         lax.psum_scatter(grad_output, "tm", scatter_dimension=0, tiled=True),
     )
     shares = (
-        lax.psum(shares[0].astype(jnp.bfloat16), "region").astype(jnp.float32),
+        jnp.sum(lax.all_gather(shares[0].astype(jnp.bfloat16), "region"), axis=0).astype(
+            jnp.float32
+        ),
         lax.psum(shares[1].astype(jnp.bfloat16), "region").astype(jnp.float32),
         lax.psum(shares[2].astype(jnp.bfloat16), "region").astype(jnp.float32),
         lax.psum(shares[3].astype(jnp.bfloat16), "region").astype(jnp.float32),

time: 589 us -> 569 us (0.966)
  the two profiles are of different devices: /device:TPU:8 before, /device:TPU:4 now
where the time goes in v1:
time: 569 us; the launch traced here: 568 us
  blocking collectives  454 us (80%)
  matrix products  43.1 us (8%)
  local copies, waits for them, and re-layouts  25.1 us (4%)
  between operations  15.4 us (3%)
  other arithmetic  12.5 us (2%)
  starting transfers between devices  9.19 us (2%)
  waiting for transfers between devices  8.41 us (1%)
    unnamed x1, blocking collectives  296 us
    psum x1, blocking collectives, per_device(): total_sq = lax.psum(local_sq, 'tm')  131 us
    dot_general x3, matrix products, energy(): jnp.einsum('...sn,...rn->...sr', scenario_vals, scenario_vals, precision=...  18.9 us
    psum x1, blocking collectives, per_device(): lax.psum(shares[1].astype(jnp.bfloat16), 'region').astype(jnp.float32)  16.5 us
  transfers between devices with their start and end apart: 7, of which 5 were waited for; matrix products, arithmetic and copies ran while one was open for 3% of the time, Pallas kernels for 0%

profile of v1, /device:TPU:4, one launch (start us, length us, event | category | flops | bytes accessed | tf_op | source)
XLA Modules:
  0.0 567.5 jit_solution(14147904439924340539)
XLA Ops:
  8.5 1.7 collective-permute-start
  10.3 1.7 multiply_reduce_fusion.1
  12.0 131.3 %psum.28 = f32[2]{0:T(128)S(1)} all-reduce(f32[2]{0:T(128)S(1)} %get-tuple-element.18), channel_id=1, replica_groups=mesh['tm'=64,'region'=4] {'tm'}, use_global_device_ids=true, to_apply=%region_2.3 | all-reduce | flops 2 | bytes 16 | tf_op jit(solution)/shard_map/psum | solution.py:86
  150.6 2.2 collective-permute-start.2
  156.3 1.7 copy.100
  158.1 1.9 copy-done.1
  160.0 6.3 %fusion.6 = f32[2,128,16,16]{3,2,1,0:T(8,128)} fusion(f32[2,128,16,256]{3,2,1,0:T(8,128)S(1)} %bitcast.164), kind=kOutput, calls=%fused_computation.9 | convolution fusion | flops 201326592 | bytes 4456448 | tf_op jit(solution)/shard_map/jvp(...sn,...rn->...sr)/dot_general | solution.py:18
  166.3 3.2 copy.60
  169.5 2.3 copy.63
  171.8 1.7 gather_fusion
  174.1 6.5 %fusion.4 = f32[2,128,1,16]{3,2,1,0:T(1,128)} fusion(f32[2,128,256,1]{2,1,0,3:T(8,128)S(1)} %bitcast.169, f32[2,128,16,256]{3,2,1,0:T(8,128)} %bitcast.165), kind=kOutput, calls=%fused_computation.7 | convolution fusion | flops 12582912 | bytes 4472832 | tf_op jit(solution)/shard_map/jvp(...sn,...n->...s)/dot_general | solution.py:21
  184.8 1.6 scatter_fusion
  186.5 2.1 copy.71
  188.7 6.9 %fusion = f32[2,128,16,256]{3,2,1,0:T(8,128)S(1)} fusion(f32[2,128,16,16]{3,2,1,0:T(8,128)} %copy.71, f32[2,128,16,256]{3,2,1,0:T(8,128)} %bitcast.166), kind=kOutput, calls=%fused_computation.3 | convolution fusion | flops 201326592 | bytes 8650752 | tf_op jit(solution)/shard_map/transpose(jvp(...sn,...rn->...sr))/dot_general | solution.py:18
  195.6 5.7 %add_add_fusion = bf16[2,128,16,256]{3,2,1,0:T(8,128)(2,1)} fusion(f32[2,128,16,256]{3,2,1,0:T(8,128)S(1)} %fusion, f32[2,128,16,16]{3,2,1,0:T(8,128)S(1)} %copy-done.3, f32[2,128,256]{2,1,0:T(8,128)S(1)} %copy-done.4, f32[2,128,16]{2,1,0:T(8,128)S(1)} %copy.62, f32[2,128,16,256]{3,2,1,0:T(8,128)S(1)} %bitcast.167), kind=kOutput, calls=%fused_computation.11 | convolution fusion | flops 205520896 | bytes 11026432 | tf_op jit(solution)/shard_map/transpose(jvp(...sn,...rn->...sr))/dot_general | solution.py:18
  201.3 4.2 reshape.36
  205.5 2.5 fusion.17
  214.4 3.2 collective-permute-done.4
  218.7 2.0 pad_maximum_fusion
  222.6 4.3 convolution_bitcast_fusion
  230.5 3.3 collective-permute-done.5
  234.1 295.9 %all-reduce.12 = (bf16[256,256]{0,1:T(8,128)(2,1)S(1)}, bf16[3,256,256]{2,1,0:T(8,128)(2,1)}, bf16[256,4096]{1,0:T(8,128)(2,1)}) all-reduce(f32[256,256]{0,1:T(8,128)S(1)} %convolution_bitcast_fusion.7, f32[3,256,256]{2,1,0:T(8,128)S(1)} %pad_maximum_fusion.1, ...), channel_id=3, replica_groups=mesh['tm'=64,'region'=4] {'tm'}, use_global_device_ids=true, to_apply=%region_6.7.clone | all-reduce | flops 1310720 | bytes 7864320
  530.2 10.1 %all-gather.1 = bf16[4,4,256]{2,1,0:T(4,128)(2,1)S(1)} all-gather(bf16[1,4,256]{2,1,0:T(4,128)(2,1)S(1)} %copy.73), channel_id=2, replica_groups=mesh['tm'=64,'region'=4] {'region'}, dimensions={0}, use_global_device_ids=true | all-gather | bytes 10240 | tf_op jit(solution)/shard_map/all_gather | solution.py:146
  544.2 16.5 %all-reduce.10 = (bf16[3,8,512]{2,1,0:T(8,128)(2,1)}, bf16[3,4,256]{2,1,0:T(4,128)(2,1)}, bf16[4,4096]{1,0:T(4,128)(2,1)}) all-reduce(bf16[3,8,512]{2,1,0:T(8,128)(2,1)S(1)} %convert_element_type.122, bf16[3,4,256]{2,1,0:T(4,128)(2,1)S(1)} %dynamic-slice_convert_fusion.2, ...), channel_id=1, replica_groups=mesh['tm'=64,'region'=4] {'region'}, use_global_device_ids=true, to_apply=%region_9.10 | all-reduce | flops 31744 | bytes 126976 | tf_op jit(solution)/shard_map/psum | solution.py:149
  (135 shorter events, 33.2 us)
Async XLA Ops:
  7.2 148.4 %copy-start = (bf16[256,4096]{1,0:T(8,128)(2,1)S(1)}, bf16[256,4096]{1,0:T(8,128)(2,1)}, u32[]{:S(2)}) copy-start(bf16[256,4096]{1,0:T(8,128)(2,1)} %param.11) | copy-start | bytes 6291460
  7.2 536.2 %reduce-scatter.4.cloned.1.call-start = ((), (), s32[]{:S(2)}) async-start(), calls=%async_computation.1 | async-start | bytes 3194880 | tf_op jit(solution)/shard_map/reduce_scatter | solution.py:141
  8.5 136.0 %collective-permute-start = (bf16[2,1,256]{2,1,0:T(2,128)(2,1)S(1)}, bf16[2,1,256]{2,1,0:T(2,128)(2,1)S(1)}, u32[]{:S(2)}, u32[]{:S(2)}) collective-permute-start(bf16[2,1,256]{2,1,0:T(2,128)(2,1)S(1)} %slice.133), channel_id=1, source_target_pairs={{0,4},{4,8},{8,12},{12,16},{16,20},{20,24},{24,28},{28,32},{32,36}... | collective-permute-start | bytes 3080 | tf_op jit(solution)/shard_map/ppermute | solution.py:12
  143.3 6.6 %copy-start.30 = (bf16[3,512,512]{2,1,0:T(8,128)(2,1)S(1)}, bf16[3,512,512]{2,1,0:T(8,128)(2,1)}, u32[]{:S(2)}) copy-start(bf16[3,512,512]{2,1,0:T(8,128)(2,1)} %param.9) | copy-start | bytes 4718596
  144.5 5.8 %copy-start.9 = (bf16[3,256,256]{2,1,0:T(8,128)(2,1)S(1)}, bf16[3,256,256]{2,1,0:T(8,128)(2,1)}, u32[]{:S(2)}) copy-start(bf16[3,256,256]{2,1,0:T(8,128)(2,1)} %param.10) | copy-start | bytes 1179652
  146.1 3.3 copy-start.13
  147.2 2.1 collective-permute-start.1
  150.2 3.9 copy-start.5
  150.4 3.3 copy-start.15
  150.6 3.1 collective-permute-start.2
  166.3 7.8 %copy-start.4 = (f32[2,128,256]{2,1,0:T(8,128)S(1)}, f32[2,128,256]{2,1,0:T(8,128)}, u32[]{:S(2)}) copy-start(f32[2,128,256]{2,1,0:T(8,128)} %param.7) | copy-start | bytes 786436
  188.7 6.9 %copy-start.2 = (f32[32,8,16,256]{3,2,1,0:T(8,128)S(1)}, f32[32,8,16,256]{3,2,1,0:T(8,128)}, u32[]{:S(2)}) copy-start(f32[32,8,16,256]{3,2,1,0:T(8,128)} %copy-done.1) | copy-start | bytes 12582916
  188.7 6.9 %copy-start.3 = (f32[2,128,16,16]{3,2,1,0:T(8,128)S(1)}, f32[2,128,16,16]{3,2,1,0:T(8,128)}, u32[]{:S(2)}) copy-start(f32[2,128,16,16]{3,2,1,0:T(8,128)} %copy.71) | copy-start | bytes 786436
  208.4 3.7 copy-start.6
  208.8 3.1 collective-permute-start.3
  210.4 3.5 copy-start.29
  212.6 5.4 copy-start.27
  212.7 4.9 collective-permute-start.4
  222.6 4.3 copy-start.18
  222.6 4.6 copy-start.16
  222.6 4.8 copy-start.21
  227.4 6.4 %copy-start.22 = (bf16[2,128,256]{2,1,0:T(8,128)(2,1)S(1)}, bf16[2,128,256]{2,1,0:T(8,128)(2,1)}, u32[]{:S(2)}) copy-start(bf16[2,128,256]{2,1,0:T(8,128)(2,1)} %param.6) | copy-start | bytes 393220
  228.9 4.9 collective-permute-start.5
  234.1 307.5 %copy-start.19 = (bf16[256,256]{1,0:T(8,128)(2,1)S(1)}, bf16[256,256]{1,0:T(8,128)(2,1)}, u32[]{:S(2)}) copy-start(bf16[256,256]{1,0:T(8,128)(2,1)} %param.8) | copy-start | bytes 393220
  (16 other events, 25.5 us)
Sparse Core Ops, SparseCore 0:
  220.8 139.8 reduce-scatter.3
